TPU v7x, 128 devices: a whole 4x4x4 slice. The times are simulated.
128 devices in a mesh: ctx: 128 (over y, x, z, core).
Axes of the slice: x: 4, y: 4, z: 4, core: 2. Of those that a mesh axis runs over, the one named last changes fastest.
Arguments:
- q_load: bfloat16 [131072, 1024], P('ctx'), may hold values from -16 to 16
- k_load: bfloat16 [131072, 128], P('ctx'), may hold values from -12 to 12
- v_load: bfloat16 [131072, 128], P('ctx'), may hold values from -6 to 6
- dest_row: int32 [131072], P('ctx'), may hold values from 0 to 131071, as said below
- doc_id: int32 [131072], P('ctx'), may hold values from 0 to 511, never falling along the last dimension, each value on 1 to 512 neighbouring positions
- grad_out: bfloat16 [131072, 1024], P('ctx'), may hold values from -6 to 6
Outputs:
- attended: bfloat16 [131072, 1024], P('ctx')
- grad_q: float32 [131072, 1024], P('ctx')
- grad_k: float32 [131072, 128], P('ctx')
- grad_v: float32 [131072, 128], P('ctx')
Inputs may be any that keep to these rules, and one draw needn't show every extreme that they name: `dest_row`: each sequence position appears once; row j of a device's 1024 loader rows has its sequence position among the 1024 positions of device j // 8. `doc_id`: document numbers never fall along the sequence and each document has 1 to 512 tokens.
All inputs are finite; a program needn't handle non-finite values.
Results may differ from a plain program's by a relative error of at most 0.03.
Values may be sent and summed in bfloat16 or wider, within the bound.
A program may use at most 128 MiB of HBM per device.

v0:
```python
import math

import jax
import jax.numpy as jnp
from jax import lax
from jax.sharding import PartitionSpec as P

BLK = 128
MAXDOC = 512


masked_value = -1e30


def passed_along(array, axis, by):
    count = lax.axis_size(axis)
    pairs = [(i, i + by) for i in range(count) if 0 <= i + by < count]
    return lax.ppermute(array, axis, pairs)


def tile_grads(pieces, offset, scaling):
    q_tile, k_tile, v_tile, grad_tile, q_docs, k_docs = pieces
    block_len = q_tile.shape[1]
    key_len = k_tile.shape[1]
    scores = (
        jnp.einsum("gihd,gjd->ghij", q_tile, k_tile, preferred_element_type=jnp.float32) * scaling
    )
    causal = jnp.arange(key_len)[None, :] - offset <= jnp.arange(block_len)[:, None]
    allowed = (q_docs[:, :, None] == k_docs[:, None, :]) & causal[None]
    scores = jnp.where(allowed[:, None], scores, masked_value)
    top_score = jnp.max(scores, axis=-1, keepdims=True)
    log_total = top_score + jnp.log(jnp.sum(jnp.exp(scores - top_score), axis=-1, keepdims=True))
    soft_w = jnp.exp(scores - log_total)
    soft_b = soft_w.astype(jnp.bfloat16)
    attended = jnp.einsum(
        "ghij,gjd->gihd", soft_b, v_tile, preferred_element_type=jnp.float32
    ).astype(jnp.bfloat16)
    delta = jnp.sum(grad_tile.astype(jnp.float32) * attended.astype(jnp.float32), axis=-1)
    delta = jnp.transpose(delta, (0, 2, 1))[..., None]
    grad_v = jnp.einsum("ghij,gihd->gjd", soft_b, grad_tile, preferred_element_type=jnp.float32)
    grad_p = jnp.einsum("gihd,gjd->ghij", grad_tile, v_tile, preferred_element_type=jnp.float32)
    grad_s = (soft_w * (grad_p - delta)).astype(jnp.bfloat16)
    grad_q = (
        jnp.einsum("ghij,gjd->gihd", grad_s, k_tile, preferred_element_type=jnp.float32) * scaling
    )
    grad_k = (
        jnp.einsum("ghij,gihd->gjd", grad_s, q_tile, preferred_element_type=jnp.float32) * scaling
    )
    return (attended, grad_q, grad_k, grad_v)


def attend(q_rows, ext_k, ext_v, ext_doc, q_doc, grad_rows, block_len, rim):
    n_rows, width = q_rows.shape
    head_dim = ext_k.shape[1]
    heads = width // head_dim
    n_blocks = n_rows // block_len
    rim_blocks = rim // block_len
    reach = rim_blocks + 1

    def windows(source):
        stacked = source.reshape((n_blocks + rim_blocks, block_len) + source.shape[1:])
        joined = jnp.stack([stacked[w : w + n_blocks] for w in range(reach)], axis=1)
        return joined.reshape((n_blocks, reach * block_len) + source.shape[1:])

    per_step = math.gcd(n_blocks, 4)
    step_count = n_blocks // per_step

    def grouped(source):
        return source.reshape((step_count, per_step) + source.shape[1:])

    pieces = (
        grouped(q_rows.reshape(n_blocks, block_len, heads, head_dim)),
        grouped(windows(ext_k)),
        grouped(windows(ext_v)),
        grouped(grad_rows.reshape(n_blocks, block_len, heads, head_dim)),
        grouped(q_doc.reshape(n_blocks, block_len)),
        grouped(windows(ext_doc)),
    )
    scaling = 1.0 / math.sqrt(head_dim)
    attended, grad_q, grad_k, grad_v = lax.map(lambda p: tile_grads(p, rim, scaling), pieces)
    attended = attended.reshape(n_rows, width)
    grad_q = grad_q.reshape(n_rows, width)
    grad_k = grad_k.reshape(n_blocks, reach, block_len, head_dim)
    grad_v = grad_v.reshape(n_blocks, reach, block_len, head_dim)
    total_k = jnp.zeros((n_blocks + rim_blocks, block_len, head_dim), jnp.float32)
    total_v = jnp.zeros((n_blocks + rim_blocks, block_len, head_dim), jnp.float32)
    for w in range(reach):
        total_k = total_k.at[w : w + n_blocks].add(grad_k[:, w])
        total_v = total_v.at[w : w + n_blocks].add(grad_v[:, w])
    return (attended, grad_q, total_k.reshape(-1, head_dim), total_v.reshape(-1, head_dim))


def body(q_load, k_load, v_load, dest_row, doc_id, grad_out):
    local_rows = q_load.shape[0]
    recv_q, recv_k, recv_v, recv_dest = (
        lax.all_to_all(q_load, "ctx", split_axis=0, concat_axis=0, tiled=True),
        lax.all_to_all(k_load, "ctx", split_axis=0, concat_axis=0, tiled=True),
        lax.all_to_all(v_load, "ctx", split_axis=0, concat_axis=0, tiled=True),
        lax.all_to_all(dest_row, "ctx", split_axis=0, concat_axis=0, tiled=True),
    )
    placed = recv_dest % local_rows
    q_seq = jnp.zeros_like(recv_q).at[placed].set(recv_q)
    k_seq = jnp.zeros_like(recv_k).at[placed].set(recv_k)
    v_seq = jnp.zeros_like(recv_v).at[placed].set(recv_v)
    doc_plus = doc_id + 1
    whole_k, whole_v, whole_doc = passed_along((k_seq, v_seq, doc_plus), "ctx", 1)
    prev_k = whole_k[local_rows - MAXDOC :]
    prev_v = whole_v[local_rows - MAXDOC :]
    prev_doc = whole_doc[local_rows - MAXDOC :]
    ext_k = jnp.concatenate([prev_k, k_seq], axis=0)
    ext_v = jnp.concatenate([prev_v, v_seq], axis=0)
    ext_doc = jnp.concatenate([prev_doc, doc_plus], axis=0)
    attended, grad_q, total_k, total_v = attend(
        q_seq, ext_k, ext_v, ext_doc, doc_plus, grad_out, BLK, MAXDOC
    )
    padding = ((local_rows - MAXDOC, 0), (0, 0))
    back_k, back_v = (
        passed_along(jnp.pad(total_k[:MAXDOC], padding).astype(jnp.bfloat16), "ctx", -1).astype(
            jnp.float32
        ),
        passed_along(jnp.pad(total_v[:MAXDOC], padding).astype(jnp.bfloat16), "ctx", -1).astype(
            jnp.float32
        ),
    )
    grad_k = total_k[MAXDOC:] + back_k
    grad_v = total_v[MAXDOC:] + back_v
    return (attended, grad_q, grad_k, grad_v)


def solution(mesh):
    in_specs = (P("ctx", None), P("ctx", None), P("ctx", None), P("ctx"), P("ctx"), P("ctx", None))
    out_specs = (P("ctx", None), P("ctx", None), P("ctx", None), P("ctx", None))
    return jax.shard_map(body, mesh=mesh, in_specs=in_specs, out_specs=out_specs, check_vma=False)
```

profile of v0, /device:TPU:9, one launch (start us, length us, event | category | flops | bytes accessed | tf_op | source)
XLA Modules:
  0.0 204.9 jit_solution(14723121897102664544)
XLA Ops:
  1.4 18.9 %all_to_all.48 = s32[128,8,1]{1,2,0:T(1,128)S(1)} all-to-all(s32[128,8,1]{1,2,0:T(1,128)S(1)} %bitcast.314), channel_id=1, replica_groups=mesh['ctx'=128] {'ctx'}, dimensions={0} | all-to-all | bytes 8192 | tf_op jit(solution)/shard_map/all_to_all | solution.py:99
  20.3 15.7 %all_to_all.49 = bf16[128,8,128]{2,1,0:T(8,128)(2,1)S(1)} all-to-all(bf16[128,8,128]{2,1,0:T(8,128)(2,1)} %bitcast.312), channel_id=1, replica_groups=mesh['ctx'=128] {'ctx'}, dimensions={0} | all-to-all | bytes 524288 | tf_op jit(solution)/shard_map/all_to_all | solution.py:97
  36.0 15.9 %all_to_all.50 = bf16[128,8,128]{2,1,0:T(8,128)(2,1)S(1)} all-to-all(bf16[128,8,128]{2,1,0:T(8,128)(2,1)} %bitcast.313), channel_id=1, replica_groups=mesh['ctx'=128] {'ctx'}, dimensions={0} | all-to-all | bytes 524288 | tf_op jit(solution)/shard_map/all_to_all | solution.py:98
  51.9 5.8 %all-to-all-start.3 = ((bf16[128,8,1024]{2,1,0:T(8,128)(2,1)}), bf16[128,8,1024]{2,1,0:T(8,128)(2,1)S(1)}, u32[]{:S(2)}, u32[]{:S(2)}) async-start(bf16[128,8,1024]{2,1,0:T(8,128)(2,1)} %bitcast.298), calls=%async_computation.3 | async-start | bytes 4194304 | tf_op jit(solution)/shard_map/all_to_all | solution.py:96
  59.1 3.2 %scatter_custom_fusion = bf16[1024,128]{1,0:T(8,128)(2,1)S(1)} fusion(s32[1024]{0:T(1024)S(1)} %bitcast.321, bf16[128,8,128]{2,1,0:T(8,128)(2,1)S(1)} %all_to_all.50, bf16[]{:T(256)} %constant.315.clone.1), kind=kCustom, calls=%fused_computation.102 | custom fusion | bytes 524290 | tf_op jit(solution)/shard_map/scatter | solution.py:104
  62.4 3.6 %collective-permute-start = (bf16[1024,128]{1,0:T(8,128)(2,1)S(1)}, bf16[1024,128]{1,0:T(8,128)(2,1)S(1)}, u32[]{:S(2)}, u32[]{:S(2)}) collective-permute-start(bf16[1024,128]{1,0:T(8,128)(2,1)S(1)} %scatter_custom_fusion), channel_id=1, source_target_pairs={{0,1},{1,2},{2,3},{3,4},{4,5},{5,6},{6,7},{7,8},{8,9},{9,10},{10,1... | collective-permute-start | bytes 786440 | tf_op jit(solution)/shard_map/ppermute | solution.py:18
  68.1 3.5 %copy.111 = bf16[128,8,8,128]{3,2,1,0:T(8,128)(2,1)} copy(bf16[128,8,8,128]{3,1,2,0:T(8,128)(2,1)} %bitcast.297) | data formatting | bytes 4194304
  71.6 11.6 %collective-permute-done.1 = s32[1024]{0:T(1024)S(1)} collective-permute-done((s32[1024]{0:T(1024)S(1)}, s32[1024]{0:T(1024)S(1)}, u32[]{:S(2)}, u32[]{:S(2)}) %collective-permute-start.1) | collective-permute-done | bytes 4128 | tf_op jit(solution)/shard_map/ppermute | solution.py:18
  83.3 3.2 %scatter_custom_fusion.1 = bf16[1024,128]{1,0:T(8,128)(2,1)S(1)} fusion(s32[1024]{0:T(1024)S(1)} %bitcast.322, bf16[128,8,128]{2,1,0:T(8,128)(2,1)S(1)} %all_to_all.49, bf16[]{:T(256)} %constant.315.clone.1), kind=kCustom, calls=%fused_computation.100 | custom fusion | bytes 524290 | tf_op jit(solution)/shard_map/scatter | solution.py:103
  86.6 4.4 %collective-permute-start.2 = (bf16[1024,128]{1,0:T(8,128)(2,1)S(1)}, bf16[1024,128]{1,0:T(8,128)(2,1)S(1)}, u32[]{:S(2)}, u32[]{:S(2)}) collective-permute-start(bf16[1024,128]{1,0:T(8,128)(2,1)S(1)} %scatter_custom_fusion.1), channel_id=1, source_target_pairs={{0,1},{1,2},{2,3},{3,4},{4,5},{5,6},{6,7},{7,8},{8,9},{9,10},{10,1... | collective-permute-start | bytes 786440 | tf_op jit(solution)/shard_map/ppermute | solution.py:18
  92.6 3.4 %collective-permute-done.2 = bf16[1024,128]{1,0:T(8,128)(2,1)S(1)} collective-permute-done((bf16[1024,128]{1,0:T(8,128)(2,1)S(1)}, bf16[1024,128]{1,0:T(8,128)(2,1)S(1)}, u32[]{:S(2)}, u32[]{:S(2)}) %collective-permute-start.2) | collective-permute-done | bytes 262176 | tf_op jit(solution)/shard_map/ppermute | solution.py:18
  97.6 6.8 %scatter_custom_fusion.2 = bf16[1024,1024]{1,0:T(8,128)(2,1)} fusion(s32[1024]{0:T(1024)S(1)} %bitcast.323, bf16[128,8,1024]{2,1,0:T(8,128)(2,1)S(1)} %all-to-all-done.3, bf16[]{:T(256)} %constant.315.clone.1), kind=kCustom, calls=%fused_computation.49 | custom fusion | bytes 4194306 | tf_op jit(solution)/shard_map/scatter | solution.py:102
  104.4 3.5 %copy.110 = bf16[128,8,8,128]{3,2,1,0:T(8,128)(2,1)} copy(bf16[128,8,8,128]{3,1,2,0:T(8,128)(2,1)} %bitcast.282) | data formatting | bytes 4194304
  108.0 73.5 %while.28 = (s32[]{:T(128)}, bf16[2,4,128,8,128]{4,3,2,1,0:T(8,128)(2,1)}, f32[2,4,128,8,128]{4,3,2,1,0:T(8,128)}, f32[2,4,640,128]{3,2,1,0:T(8,128)}, f32[2,4,6...) while((s32[]{:T(128)}, ...), condition=%wide.region_7.8_spmd, body=%wide.region_3.7_spmd.sunk | while | flops 4085785088 | bytes 213116304 | solution.py:80
  111.2 2.7 %fusion.81 = (f32[4,8,128]{2,1,0:T(8,128)S(1)}, f32[4,640,128,8]{2,1,3,0:T(8,128)S(1)}) fusion(pred[4,128,640]{1,2,0:T(8,128)(4,1)S(1)} %compare_and_fusion.2, bf16[1,4,128,8,128]{4,3,2,1,0:T(8,128)(2,1)S(1)} %get-tuple-element.404, bf16[2,4,640,128]{3,2,1,0:T(8,128)(2,1)} %get-tuple-element.441, s32[]{:T(128)S(6)} %copy.150), kind=kOutput, calls=%fused_computation.10.clone.1 | convolution fusion | flops 678948864 | bytes 12533764 | tf_op jit(solution)/shard_map/while/body/eval_jaxpr/gihd,gjd->ghij/dot_general | solution.py:26
  117.9 3.7 %multiply_reduce_fusion.2 = (f32[4,128,8]{1,2,0:T(8,128)S(1)}, bf16[4,128,8,128]{3,1,2,0:T(8,128)(2,1)}) fusion(bf16[1,4,128,8,128]{2,4,3,1,0:T(8,128)(2,1)S(1)} %copy.130, f32[4,640,128,8]{2,1,3,0:T(8,128)S(1)} %get-tuple-element.405, f32[4,8,128]{2,1,0:T(8,128)S(1)} %log_add_fusion.2, pred[4,128,640]{1,2,0:T(8,128)(4,1)S(1)} %compare_and_fusion.2, ...), kind=kOutput, calls=%fused_computation.12.clone.1 | convolution fusion | flops 684191744 | bytes 13598724 | tf_op jit(solution)/shard_map/while/body/eval_jaxpr/ghij,gjd->gihd/dot_general | solution.py:35
  124.3 7.9 %fusion.84 = f32[2,4,640,128]{3,2,1,0:T(8,128)} fusion(f32[2,4,640,128]{3,2,1,0:T(8,128)} %get-tuple-element.425, s32[]{:T(128)S(6)} %copy.150, bf16[1,4,128,8,128]{2,4,3,1,0:T(8,128)(2,1)S(1)} %copy.130, f32[4,640,128,8]{2,1,3,0:T(8,128)} %copy-done, f32[4,8,128]{2,1,0:T(8,128)S(1)} %log_add_fusion.2, pred[4,128,640]{1,2,0:T(8,128)(4,1)S(1)} %compare_and_fusion.2), kind=kOutput, calls=%fused_computation.15.clone.1 | convolution fusion | flops 681574400 | bytes 13189124 | tf_op jit(solution)/shard_map/while/body/eval_jaxpr/ghij,gihd->gjd/dot_general | solution.py:40
  132.3 3.4 %fusion.82 = bf16[4,8,128,640]{2,3,1,0:T(8,128)(2,1)S(1)} fusion(f32[4,640,128,8]{2,1,3,0:T(8,128)S(1)} %bitcast.277, f32[4,8,128]{2,1,0:T(8,128)S(1)} %bitcast.324, f32[4,8,128]{2,1,0:T(8,128)S(1)} %log_add_fusion.2, pred[4,128,640]{1,2,0:T(8,128)(4,1)S(1)} %compare_and_fusion.2, bf16[1,4,128,8,128]{2,4,3,1,0:T(8,128)(2,1)S(1)} %copy.130, ...), kind=kOutput, calls=%fused_computation.5.clone.1 | convolution fusion | flops 686817280 | bytes 17793028 | tf_op jit(solution)/shard_map/while/body/eval_jaxpr/gihd,gjd->ghij/dot_general | solution.py:41
  147.9 2.7 %fusion.81 = (f32[4,8,128]{2,1,0:T(8,128)S(1)}, f32[4,640,128,8]{2,1,3,0:T(8,128)S(1)}) fusion(pred[4,128,640]{1,2,0:T(8,128)(4,1)S(1)} %compare_and_fusion.2, bf16[1,4,128,8,128]{4,3,2,1,0:T(8,128)(2,1)S(1)} %get-tuple-element.404, bf16[2,4,640,128]{3,2,1,0:T(8,128)(2,1)} %get-tuple-element.441, s32[]{:T(128)S(6)} %copy.150), kind=kOutput, calls=%fused_computation.10.clone.1 | convolution fusion | flops 678948864 | bytes 12533764 | tf_op jit(solution)/shard_map/while/body/eval_jaxpr/gihd,gjd->ghij/dot_general | solution.py:26
  154.6 3.7 %multiply_reduce_fusion.2 = (f32[4,128,8]{1,2,0:T(8,128)S(1)}, bf16[4,128,8,128]{3,1,2,0:T(8,128)(2,1)}) fusion(bf16[1,4,128,8,128]{2,4,3,1,0:T(8,128)(2,1)S(1)} %copy.130, f32[4,640,128,8]{2,1,3,0:T(8,128)S(1)} %get-tuple-element.405, f32[4,8,128]{2,1,0:T(8,128)S(1)} %log_add_fusion.2, pred[4,128,640]{1,2,0:T(8,128)(4,1)S(1)} %compare_and_fusion.2, ...), kind=kOutput, calls=%fused_computation.12.clone.1 | convolution fusion | flops 684191744 | bytes 13598724 | tf_op jit(solution)/shard_map/while/body/eval_jaxpr/ghij,gjd->gihd/dot_general | solution.py:35
  161.0 7.9 %fusion.84 = f32[2,4,640,128]{3,2,1,0:T(8,128)} fusion(f32[2,4,640,128]{3,2,1,0:T(8,128)} %get-tuple-element.425, s32[]{:T(128)S(6)} %copy.150, bf16[1,4,128,8,128]{2,4,3,1,0:T(8,128)(2,1)S(1)} %copy.130, f32[4,640,128,8]{2,1,3,0:T(8,128)} %copy-done, f32[4,8,128]{2,1,0:T(8,128)S(1)} %log_add_fusion.2, pred[4,128,640]{1,2,0:T(8,128)(4,1)S(1)} %compare_and_fusion.2), kind=kOutput, calls=%fused_computation.15.clone.1 | convolution fusion | flops 681574400 | bytes 13189124 | tf_op jit(solution)/shard_map/while/body/eval_jaxpr/ghij,gihd->gjd/dot_general | solution.py:40
  169.0 3.5 %fusion.82 = bf16[4,8,128,640]{2,3,1,0:T(8,128)(2,1)S(1)} fusion(f32[4,640,128,8]{2,1,3,0:T(8,128)S(1)} %bitcast.277, f32[4,8,128]{2,1,0:T(8,128)S(1)} %bitcast.324, f32[4,8,128]{2,1,0:T(8,128)S(1)} %log_add_fusion.2, pred[4,128,640]{1,2,0:T(8,128)(4,1)S(1)} %compare_and_fusion.2, bf16[1,4,128,8,128]{2,4,3,1,0:T(8,128)(2,1)S(1)} %copy.130, ...), kind=kOutput, calls=%fused_computation.5.clone.1 | convolution fusion | flops 686817280 | bytes 17793028 | tf_op jit(solution)/shard_map/while/body/eval_jaxpr/gihd,gjd->ghij/dot_general | solution.py:41
  184.3 11.0 %collective-permute-start.4 = (bf16[1024,128]{1,0:T(8,128)(2,1)S(1)}, bf16[1024,128]{1,0:T(8,128)(2,1)S(1)}, u32[]{:S(2)}, u32[]{:S(2)}) collective-permute-start(bf16[1024,128]{1,0:T(8,128)(2,1)S(1)} %pad.32), channel_id=1, source_target_pairs={{1,0},{2,1},{3,2},{4,3},{5,4},{6,5},{7,6},{8,7},{9,8},{10,9},{11,1... | collective-permute-start | bytes 786440 | tf_op jit(solution)/shard_map/ppermute | solution.py:18
  200.2 3.0 %copy.121 = f32[128,8,8,128]{3,1,2,0:T(8,128)} copy(f32[128,8,8,128]{3,2,1,0:T(8,128)S(1)} %bitcast.283) | data formatting | bytes 8388608
  (133 shorter events, 54.3 us)
Async XLA Ops:
  36.0 30.0 %copy-start.10 = (s32[1024]{0:T(1024)S(1)}, s32[1024]{0:T(1024)}, u32[]{:S(2)}) copy-start(s32[1024]{0:T(1024)} %param.32) | copy-start | bytes 12292
  51.9 45.7 %all-to-all-start.3 = ((bf16[128,8,1024]{2,1,0:T(8,128)(2,1)}), bf16[128,8,1024]{2,1,0:T(8,128)(2,1)S(1)}, u32[]{:S(2)}, u32[]{:S(2)}) async-start(bf16[128,8,1024]{2,1,0:T(8,128)(2,1)} %bitcast.298), calls=%async_computation.3 | async-start | bytes 4194304 | tf_op jit(solution)/shard_map/all_to_all | solution.py:96
  62.4 28.6 %collective-permute-start = (bf16[1024,128]{1,0:T(8,128)(2,1)S(1)}, bf16[1024,128]{1,0:T(8,128)(2,1)S(1)}, u32[]{:S(2)}, u32[]{:S(2)}) collective-permute-start(bf16[1024,128]{1,0:T(8,128)(2,1)S(1)} %scatter_custom_fusion), channel_id=1, source_target_pairs={{0,1},{1,2},{2,3},{3,4},{4,5},{5,6},{6,7},{7,8},{8,9},{9,10},{10,1... | collective-permute-start | bytes 786440 | tf_op jit(solution)/shard_map/ppermute | solution.py:18
  66.0 17.2 %collective-permute-start.1 = (s32[1024]{0:T(1024)S(1)}, s32[1024]{0:T(1024)S(1)}, u32[]{:S(2)}, u32[]{:S(2)}) collective-permute-start(s32[1024]{0:T(1024)S(1)} %broadcast_add_fusion), channel_id=1, source_target_pairs={{0,1},{1,2},{2,3},{3,4},{4,5},{5,6},{6,7},{7,8},{8,9},{9,10},{10,1... | collective-permute-start | bytes 12296 | tf_op jit(solution)/shard_map/ppermute | solution.py:18
  86.6 9.4 %collective-permute-start.2 = (bf16[1024,128]{1,0:T(8,128)(2,1)S(1)}, bf16[1024,128]{1,0:T(8,128)(2,1)S(1)}, u32[]{:S(2)}, u32[]{:S(2)}) collective-permute-start(bf16[1024,128]{1,0:T(8,128)(2,1)S(1)} %scatter_custom_fusion.1), channel_id=1, source_target_pairs={{0,1},{1,2},{2,3},{3,4},{4,5},{5,6},{6,7},{7,8},{8,9},{9,10},{10,1... | collective-permute-start | bytes 786440 | tf_op jit(solution)/shard_map/ppermute | solution.py:18
  113.9 4.0 %copy-start = (f32[4,640,128,8]{2,1,3,0:T(8,128)}, f32[4,640,128,8]{2,1,3,0:T(8,128)S(1)}, u32[]{:S(2)}) copy-start(f32[4,640,128,8]{2,1,3,0:T(8,128)S(1)} %get-tuple-element.405) | copy-start | bytes 31457284 | tf_op jit(solution)/shard_map/while
  113.9 4.0 %copy-start.8 = (bf16[2,4,640,128]{3,2,1,0:T(8,128)(2,1)S(1)}, bf16[2,4,640,128]{3,2,1,0:T(8,128)(2,1)}, u32[]{:S(2)}) copy-start(bf16[2,4,640,128]{3,2,1,0:T(8,128)(2,1)} %get-tuple-element.438) | copy-start | bytes 3932164 | tf_op jit(solution)/shard_map/while
  123.2 9.0 %slice-start = ((s8[10485760]{0:T(1024)(128)(4,1)}), s8[4194304]{0:T(1024)(128)(4,1)S(1)}, s32[]{:S(2)}) async-start(s8[10485760]{0:T(1024)(128)(4,1)} %bitcast.276), calls=%async_computation.4 | async-start | bytes 8388608 | tf_op jit(solution)/shard_map/while
  124.3 7.9 %slice-start.1 = ((s8[10485760]{0:T(1024)(128)(4,1)}), s8[4194304]{0:T(1024)(128)(4,1)S(1)}, s32[]{:S(2)}) async-start(s8[10485760]{0:T(1024)(128)(4,1)} %bitcast.276), calls=%async_computation.5 | async-start | bytes 8388608 | tf_op jit(solution)/shard_map/while
  124.3 7.9 %slice-start.2 = ((s8[10485760]{0:T(1024)(128)(4,1)}), s8[2097152]{0:T(1024)(128)(4,1)S(1)}, s32[]{:S(2)}) async-start(s8[10485760]{0:T(1024)(128)(4,1)} %bitcast.276), calls=%async_computation.6 | async-start | bytes 4194304 | tf_op jit(solution)/shard_map/while
  124.3 7.9 %copy-start.9 = (bf16[2,4,640,128]{3,2,1,0:T(8,128)(2,1)S(1)}, bf16[2,4,640,128]{3,2,1,0:T(8,128)(2,1)}, u32[]{:S(2)}) copy-start(bf16[2,4,640,128]{3,2,1,0:T(8,128)(2,1)} %get-tuple-element.438) | copy-start | bytes 3932164 | tf_op jit(solution)/shard_map/while
  132.2 3.5 %copy-start.4 = (f32[2,4,640,128]{3,2,1,0:T(8,128)S(1)}, f32[2,4,640,128]{3,2,1,0:T(8,128)}, u32[]{:S(2)}) copy-start(f32[2,4,640,128]{3,2,1,0:T(8,128)} %get-tuple-element.424) | copy-start | bytes 7864324 | tf_op jit(solution)/shard_map/while
  150.6 4.0 %copy-start = (f32[4,640,128,8]{2,1,3,0:T(8,128)}, f32[4,640,128,8]{2,1,3,0:T(8,128)S(1)}, u32[]{:S(2)}) copy-start(f32[4,640,128,8]{2,1,3,0:T(8,128)S(1)} %get-tuple-element.405) | copy-start | bytes 31457284 | tf_op jit(solution)/shard_map/while
  150.6 4.0 %copy-start.8 = (bf16[2,4,640,128]{3,2,1,0:T(8,128)(2,1)S(1)}, bf16[2,4,640,128]{3,2,1,0:T(8,128)(2,1)}, u32[]{:S(2)}) copy-start(bf16[2,4,640,128]{3,2,1,0:T(8,128)(2,1)} %get-tuple-element.438) | copy-start | bytes 3932164 | tf_op jit(solution)/shard_map/while
  160.0 9.0 %slice-start = ((s8[10485760]{0:T(1024)(128)(4,1)}), s8[4194304]{0:T(1024)(128)(4,1)S(1)}, s32[]{:S(2)}) async-start(s8[10485760]{0:T(1024)(128)(4,1)} %bitcast.276), calls=%async_computation.4 | async-start | bytes 8388608 | tf_op jit(solution)/shard_map/while
  161.0 7.9 %slice-start.1 = ((s8[10485760]{0:T(1024)(128)(4,1)}), s8[4194304]{0:T(1024)(128)(4,1)S(1)}, s32[]{:S(2)}) async-start(s8[10485760]{0:T(1024)(128)(4,1)} %bitcast.276), calls=%async_computation.5 | async-start | bytes 8388608 | tf_op jit(solution)/shard_map/while
  161.0 7.9 %slice-start.2 = ((s8[10485760]{0:T(1024)(128)(4,1)}), s8[2097152]{0:T(1024)(128)(4,1)S(1)}, s32[]{:S(2)}) async-start(s8[10485760]{0:T(1024)(128)(4,1)} %bitcast.276), calls=%async_computation.6 | async-start | bytes 4194304 | tf_op jit(solution)/shard_map/while
  161.0 7.9 %copy-start.9 = (bf16[2,4,640,128]{3,2,1,0:T(8,128)(2,1)S(1)}, bf16[2,4,640,128]{3,2,1,0:T(8,128)(2,1)}, u32[]{:S(2)}) copy-start(bf16[2,4,640,128]{3,2,1,0:T(8,128)(2,1)} %get-tuple-element.438) | copy-start | bytes 3932164 | tf_op jit(solution)/shard_map/while
  169.0 3.5 %copy-start.4 = (f32[2,4,640,128]{3,2,1,0:T(8,128)S(1)}, f32[2,4,640,128]{3,2,1,0:T(8,128)}, u32[]{:S(2)}) copy-start(f32[2,4,640,128]{3,2,1,0:T(8,128)} %get-tuple-element.424) | copy-start | bytes 7864324 | tf_op jit(solution)/shard_map/while
  172.5 3.1 %copy-start.1 = (bf16[2,4,640,128]{3,2,1,0:T(8,128)(2,1)S(1)}, bf16[2,4,640,128]{3,2,1,0:T(8,128)(2,1)}, u32[]{:S(2)}) copy-start(bf16[2,4,640,128]{3,2,1,0:T(8,128)(2,1)} %get-tuple-element.441) | copy-start | bytes 3932164 | tf_op jit(solution)/shard_map/while
  183.9 11.4 %copy-start.6 = (f32[2,4,640,128]{3,2,1,0:T(8,128)S(1)}, f32[2,4,640,128]{3,2,1,0:T(8,128)}, u32[]{:S(2)}) copy-start(f32[2,4,640,128]{3,2,1,0:T(8,128)} %get-tuple-element.266) | copy-start | bytes 7864324
  184.3 18.9 %collective-permute-start.4 = (bf16[1024,128]{1,0:T(8,128)(2,1)S(1)}, bf16[1024,128]{1,0:T(8,128)(2,1)S(1)}, u32[]{:S(2)}, u32[]{:S(2)}) collective-permute-start(bf16[1024,128]{1,0:T(8,128)(2,1)S(1)} %pad.32), channel_id=1, source_target_pairs={{1,0},{2,1},{3,2},{4,3},{5,4},{6,5},{7,6},{8,7},{9,8},{10,9},{11,1... | collective-permute-start | bytes 786440 | tf_op jit(solution)/shard_map/ppermute | solution.py:18
  196.0 4.2 %copy-start.2 = (f32[2,4,128,8,128]{4,3,2,1,0:T(8,128)S(1)}, f32[2,4,128,8,128]{4,3,2,1,0:T(8,128)}, u32[]{:S(2)}) copy-start(f32[2,4,128,8,128]{4,3,2,1,0:T(8,128)} %get-tuple-element.265) | copy-start | bytes 12582916
  196.0 8.1 %collective-permute-start.3 = (bf16[1024,128]{1,0:T(8,128)(2,1)S(1)}, bf16[1024,128]{1,0:T(8,128)(2,1)S(1)}, u32[]{:S(2)}, u32[]{:S(2)}) collective-permute-start(bf16[1024,128]{1,0:T(8,128)(2,1)S(1)} %pad.31), channel_id=1, source_target_pairs={{1,0},{2,1},{3,2},{4,3},{5,4},{6,5},{7,6},{8,7},{9,8},{10,9},{11,1... | collective-permute-start | bytes 786440 | tf_op jit(solution)/shard_map/ppermute | solution.py:18
  (5 other events, 11.3 us)
where the time goes:
time: 206 us; the launch traced here: 205 us
  local copies, waits for them, and re-layouts  54.6 us (27%)
  blocking collectives  50.5 us (25%)
  matrix products  43.3 us (21%)
  starting transfers between devices  29 us (14%)
  waiting for transfers between devices  15.1 us (7%)
  other arithmetic  10.9 us (5%)
    ppermute x5, starting transfers between devices, passed_along(): return lax.ppermute(array, axis, pairs)  23.3 us
    all_to_all x1, blocking collectives, body(): lax.all_to_all(dest_row, 'ctx', split_axis=0, concat_axis=0, tiled=True)  18.9 us
    all_to_all x1, blocking collectives, body(): lax.all_to_all(v_load, 'ctx', split_axis=0, concat_axis=0, tiled=True)  15.9 us
    dot_general x2, matrix products, tile_grads(): jnp.einsum('ghij,gihd->gjd', soft_b, grad_tile, preferred_element_type=jn...  15.8 us
    all_to_all x1, blocking collectives, body(): lax.all_to_all(k_load, 'ctx', split_axis=0, concat_axis=0, tiled=True)  15.7 us
    ppermute x5, waiting for transfers between devices, passed_along(): return lax.ppermute(array, axis, pairs)  15.1 us
    dynamic_update_slice x8, local copies, waits for them, and re-layouts, attend(): lax.map(lambda p: tile_grads(p, rim, scaling), pieces)  12.5 us
    unnamed x22, local copies, waits for them, and re-layouts  12.3 us
  transfers between devices with their start and end apart: 6, of which 2 were waited for; matrix products, arithmetic and copies ran while one was open for 10% of the time, Pallas kernels for 0%

commit v1 on v0

v1 whole, which is shorter than its diff:
```python
import functools
import math

import jax
import jax.numpy as jnp
from jax import lax
from jax.experimental import pallas as pl
from jax.experimental.pallas import tpu as pltpu
from jax.sharding import PartitionSpec as P

BLK = 128
MAXDOC = 512
REACH = MAXDOC // BLK
MASKED = -1e30

NT = (((1,), (1,)), ((), ()))


def dot(a, b):
    return jnp.dot(a, b, preferred_element_type=jnp.float32)


def dot_nt(a, b):
    return lax.dot_general(a, b, NT, preferred_element_type=jnp.float32)


def identity(n):
    rows = lax.broadcasted_iota(jnp.int32, (n, n), 0)
    cols = lax.broadcasted_iota(jnp.int32, (n, n), 1)
    return jnp.where(rows == cols, 1.0, 0.0).astype(jnp.bfloat16)


def passed_along(array, axis, by):
    count = lax.axis_size(axis)
    pairs = [(i, i + by) for i in range(count) if 0 <= i + by < count]
    return lax.ppermute(array, axis, pairs)


def slots_of(pos_cols):
    lane = lax.broadcasted_iota(jnp.int32, (8, BLK), 1)
    weights = jnp.where(lane == 0, 32.0, jnp.where(lane == 1, 1.0, 0.0)).astype(jnp.bfloat16)
    return dot_nt(weights, pos_cols)[0:1].astype(jnp.int32)


def selection(slots, first):
    want = first + lax.broadcasted_iota(jnp.int32, (BLK, slots.shape[1]), 0)
    return jnp.where(slots == want, 1.0, 0.0).astype(jnp.bfloat16)


def place_kernel(n_rows, recv_ref, kv_ref, slot_ref):
    slots = slots_of(recv_ref[:, 2 * BLK :])
    slot_ref[...] = jnp.broadcast_to(slots, slot_ref.shape)
    for i in range(n_rows // BLK):
        chosen = selection(slots, i * BLK)
        kv_ref[i * BLK : (i + 1) * BLK, :] = dot(chosen, recv_ref[:, : 2 * BLK]).astype(jnp.bfloat16)


def place(recv):
    n_rows = recv.shape[0]
    return pl.pallas_call(
        functools.partial(place_kernel, n_rows),
        out_shape=(
            jax.ShapeDtypeStruct((n_rows, 2 * BLK), jnp.bfloat16),
            jax.ShapeDtypeStruct((8, n_rows), jnp.int32),
        ),
        in_specs=[pl.BlockSpec(memory_space=pltpu.VMEM)],
        out_specs=(pl.BlockSpec(memory_space=pltpu.VMEM),) * 2,
        name="place_kv",
    )(recv)


def attend_kernel(
    n_blocks,
    heads,
    group,
    docs_smem,
    q_ref,
    slot_ref,
    kv_ref,
    halo_ref,
    doc_ref,
    grad_ref,
    att_ref,
    gq_ref,
    gk_ref,
    gv_ref,
    q_s,
    k_s,
    v_s,
    bias_s,
    dk_s,
    dv_s,
):
    step = pl.program_id(0)
    rim = REACH * BLK
    scale = 1.0 / math.sqrt(BLK)
    to_log2 = scale * math.log2(math.e)

    @pl.when(step == 0)
    def _():
        k_s[0:rim, :] = halo_ref[:, :BLK]
        k_s[rim:, :] = kv_ref[:, :BLK]
        v_s[0:rim, 0:BLK] = halo_ref[:, BLK:]
        v_s[rim:, 0:BLK] = kv_ref[:, BLK:]
        v_s[:, BLK:] = jnp.ones((rim + n_blocks * BLK, BLK), jnp.bfloat16)
        dk_s[...] = jnp.zeros_like(dk_s)
        dv_s[...] = jnp.zeros_like(dv_s)

    chosen = selection(slot_ref[0:1, :], step * BLK)
    q_s[...] = dot(chosen, q_ref[...]).astype(jnp.bfloat16)

    own = docs_smem[(step + REACH) * BLK]
    reach = jnp.int32(1)
    for w in range(1, REACH + 1):
        reach = reach + jnp.where(docs_smem[(step + REACH - w + 1) * BLK - 1] == own, 1, 0)

    q_docs = jnp.transpose(jnp.broadcast_to(doc_ref[pl.ds(step + REACH, 1), :], (BLK, BLK)))

    def run(n):
        width = n * BLK
        first = step + REACH + 1 - n
        start = pl.multiple_of(first * BLK, BLK)
        keys = pl.ds(start, width)
        row = lax.broadcasted_iota(jnp.int32, (BLK, BLK), 0)
        col = lax.broadcasted_iota(jnp.int32, (BLK, BLK), 1)
        for w in range(n):
            same = q_docs == doc_ref[pl.ds(first + w, 1), :]
            if w == n - 1:
                same = same & (col <= row)
            bias_s[:, w * BLK : (w + 1) * BLK] = jnp.where(same, 0.0, MASKED)
        eye = identity(BLK)
        ones = jnp.ones((BLK, BLK), jnp.bfloat16)
        rows = group * BLK

        def piece(g):
            at = [g * group * BLK + h * BLK for h in range(group)]
            q = jnp.concatenate([q_s[:, a : a + BLK] for a in at], axis=0)
            grad = jnp.concatenate([grad_ref[:, a : a + BLK] for a in at], axis=0)
            scores = dot_nt(q, k_s[keys, :]) * to_log2
            scores = (
                scores.reshape(group, BLK, width) + bias_s[:, :width][None]
            ).reshape(rows, width)
            top = jnp.max(scores, axis=-1, keepdims=True)
            weight = jnp.exp2(scores - top)
            weight_b = weight.astype(jnp.bfloat16)
            both = dot(weight_b, v_s[keys, :])
            inverse = 1.0 / both[:, BLK:]
            attended = (both[:, :BLK] * inverse).astype(jnp.bfloat16)
            grad_n = grad.astype(jnp.float32) * inverse
            product = grad_n * attended.astype(jnp.float32)
            delta = dot(product.astype(jnp.bfloat16), ones)
            grad_n = grad_n.astype(jnp.bfloat16)
            grad_p = dot_nt(grad_n, v_s[keys, 0:BLK])
            grad_s = jnp.concatenate(
                [
                    weight[:, w * BLK : (w + 1) * BLK]
                    * (grad_p[:, w * BLK : (w + 1) * BLK] - delta)
                    for w in range(n)
                ],
                axis=1,
            ).astype(jnp.bfloat16)
            grad_q = dot(grad_s, k_s[keys, :]) * scale
            for h, a in enumerate(at):
                att_ref[:, a : a + BLK] = attended[h * BLK : (h + 1) * BLK]
                gq_ref[:, a : a + BLK] = grad_q[h * BLK : (h + 1) * BLK]
            grad_t = dot_nt(eye, grad_n).astype(jnp.bfloat16)
            q_t = dot_nt(eye, q).astype(jnp.bfloat16)
            dv_s[:, keys] += dot(grad_t, weight_b)
            dk_s[:, keys] += dot(q_t, grad_s)

        for g in range(heads // group):
            piece(g)

    for n in range(1, REACH + 2):
        pl.when(reach == n)(functools.partial(run, n))

    @pl.when(step == n_blocks - 1)
    def _():
        for b in range(n_blocks + REACH):
            part = slice(b * BLK, (b + 1) * BLK)
            gk_ref[part, :] = jnp.transpose(dk_s[:, part]) * scale
            gv_ref[part, :] = jnp.transpose(dv_s[:, part])


def attend(q_recv, slots, kv_seq, halo, ext_doc, grad_out):
    n_rows, width = q_recv.shape
    heads = width // BLK
    n_blocks = n_rows // BLK
    ext = n_rows + MAXDOC
    whole = lambda shape: pl.BlockSpec(shape, lambda i, docs: (0, 0))
    per_block = pl.BlockSpec((BLK, width), lambda i, docs: (i, 0))
    return pl.pallas_call(
        functools.partial(attend_kernel, n_blocks, heads, 2),
        out_shape=(
            jax.ShapeDtypeStruct((n_rows, width), jnp.bfloat16),
            jax.ShapeDtypeStruct((n_rows, width), jnp.float32),
            jax.ShapeDtypeStruct((ext, BLK), jnp.float32),
            jax.ShapeDtypeStruct((ext, BLK), jnp.float32),
        ),
        grid_spec=pltpu.PrefetchScalarGridSpec(
            num_scalar_prefetch=1,
            grid=(n_blocks,),
            in_specs=[
                whole((n_rows, width)),
                whole((8, n_rows)),
                whole((n_rows, 2 * BLK)),
                whole((MAXDOC, 2 * BLK)),
                whole((ext // BLK, BLK)),
                per_block,
            ],
            out_specs=[per_block, per_block, whole((ext, BLK)), whole((ext, BLK))],
            scratch_shapes=[
                pltpu.VMEM((BLK, width), jnp.bfloat16),
                pltpu.VMEM((ext, BLK), jnp.bfloat16),
                pltpu.VMEM((ext, 2 * BLK), jnp.bfloat16),
                pltpu.VMEM((BLK, MAXDOC + BLK), jnp.float32),
                pltpu.VMEM((BLK, ext), jnp.float32),
                pltpu.VMEM((BLK, ext), jnp.float32),
            ],
        ),
        compiler_params=pltpu.CompilerParams(
            dimension_semantics=("arbitrary",), vmem_limit_bytes=40 << 20
        ),
        name="attend",
    )(ext_doc, q_recv, slots, kv_seq, halo, ext_doc.reshape(ext // BLK, BLK), grad_out)


def position_columns(dest_row, n_rows):
    local = (dest_row % n_rows)[:, None]
    lane = lax.broadcasted_iota(jnp.int32, (n_rows, BLK), 1)
    parts = jnp.where(lane == 0, local // 32, jnp.where(lane == 1, local % 32, 0))
    return parts.astype(jnp.bfloat16)


def exchange(array):
    return lax.all_to_all(array, "ctx", split_axis=0, concat_axis=0, tiled=True)


def body(q_load, k_load, v_load, dest_row, doc_id, grad_out):
    n_rows, width = q_load.shape
    doc_plus = doc_id + 1
    prev_doc = passed_along(doc_plus[n_rows - MAXDOC :], "ctx", 1)
    ext_doc = jnp.concatenate([prev_doc, doc_plus])
    recv_kv = exchange(
        jnp.concatenate([k_load, v_load, position_columns(dest_row, n_rows)], axis=1)
    )
    recv_q = exchange(q_load)
    kv_seq, slots = place(recv_kv)
    halo = passed_along(kv_seq[n_rows - MAXDOC :], "ctx", 1)
    attended, grad_q, total_k, total_v = attend(
        recv_q, slots, kv_seq, halo, ext_doc, grad_out
    )
    back = passed_along(
        jnp.concatenate([total_k[:MAXDOC], total_v[:MAXDOC]], axis=1).astype(jnp.bfloat16),
        "ctx",
        -1,
    ).astype(jnp.float32)
    padding = ((n_rows - MAXDOC, 0), (0, 0))
    grad_k = total_k[MAXDOC:] + jnp.pad(back[:, :BLK], padding)
    grad_v = total_v[MAXDOC:] + jnp.pad(back[:, BLK:], padding)
    return (attended, grad_q, grad_k, grad_v)


def solution(mesh):
    in_specs = (P("ctx", None), P("ctx", None), P("ctx", None), P("ctx"), P("ctx"), P("ctx", None))
    out_specs = (P("ctx", None), P("ctx", None), P("ctx", None), P("ctx", None))
    return jax.shard_map(body, mesh=mesh, in_specs=in_specs, out_specs=out_specs, check_vma=False)
```

time: 206 us -> 114 us (0.55)
  local copies, waits for them, and re-layouts: 54.6 us -> 4.43 us
  matrix products: 43.3 us -> 0 us
  Pallas kernels: 0 us -> 38 us
  blocking collectives: 50.5 us -> 25.9 us
  starting transfers between devices: 29 us -> 13.6 us
  waiting for transfers between devices: 15.1 us -> 25.7 us
  other arithmetic: 10.9 us -> 3.93 us
    dot_general x12 -> x0, matrix products: 43.3 us -> none  [the longest x2 15.8 us: tile_grads(): jnp.einsum('ghij,gihd->gjd', soft_b, grad_tile, preferred_element_type=jn...]
    pallas_call x0 -> x2, Pallas kernels: none -> 38 us  [the longest x1 35.2 us: attend(): pl.pallas_call(functools.partial(attend_kernel, n_blocks, heads, 2), out_...]
    all_to_all x3 -> x1, blocking collectives: 50.5 us -> 25.9 us  [exchange(): return lax.all_to_all(array, 'ctx', split_axis=0, concat_axis=0, tiled=True)]
    ppermute x5 -> x3, starting transfers between devices: 23.3 us -> 7.59 us  [passed_along(): return lax.ppermute(array, axis, pairs)]
    scatter x3 -> x0, local copies, waits for them, and re-layouts: 13.3 us -> none  [the longest x1 6.81 us: body(): q_seq = jnp.zeros_like(recv_q).at[placed].set(recv_q)]
    dynamic_update_slice x8 -> x0, local copies, waits for them, and re-layouts: 12.5 us -> none  [attend(): lax.map(lambda p: tile_grads(p, rim, scaling), pieces)]
    unnamed x22 -> x8, local copies, waits for them, and re-layouts: 12.3 us -> 3.39 us
    ppermute x5 -> x3, waiting for transfers between devices: 15.1 us -> 21.9 us  [passed_along(): return lax.ppermute(array, axis, pairs)]
  transfers between devices with their start and end apart: 6 -> 4, of which waited for: 2 -> 3; matrix products, arithmetic and copies ran while one was open for 10% -> 1% of each run, Pallas kernels for 0% -> 2%
where the time goes in v1:
time: 114 us; the launch traced here: 112 us
  Pallas kernels  38 us (33%)
  blocking collectives  25.9 us (23%)
  waiting for transfers between devices  25.7 us (23%)
  starting transfers between devices  13.6 us (12%)
  local copies, waits for them, and re-layouts  4.43 us (4%)
  other arithmetic  3.93 us (3%)
    pallas_call x1, Pallas kernels, attend(): pl.pallas_call(functools.partial(attend_kernel, n_blocks, heads, 2), out_...  35.2 us
    all_to_all x1, blocking collectives, exchange(): return lax.all_to_all(array, 'ctx', split_axis=0, concat_axis=0, tiled=True)  25.9 us
    ppermute x3, waiting for transfers between devices, passed_along(): return lax.ppermute(array, axis, pairs)  21.9 us
    ppermute x3, starting transfers between devices, passed_along(): return lax.ppermute(array, axis, pairs)  7.59 us
    all_to_all x1, starting transfers between devices, exchange(): return lax.all_to_all(array, 'ctx', split_axis=0, concat_axis=0, tiled=True)  5.97 us
    all_to_all x1, waiting for transfers between devices, exchange(): return lax.all_to_all(array, 'ctx', split_axis=0, concat_axis=0, tiled=True)  3.85 us
    unnamed x8, local copies, waits for them, and re-layouts  3.39 us
    pallas_call x1, Pallas kernels, place(): pl.pallas_call(functools.partial(place_kernel, n_rows), out_shape=(jax.Sh...  2.77 us
  transfers between devices with their start and end apart: 4, of which 3 were waited for; matrix products, arithmetic and copies ran while one was open for 1% of the time, Pallas kernels for 2%

profile of v1, /device:TPU:9, one launch (start us, length us, event | category | flops | bytes accessed | tf_op | source)
XLA Modules:
  0.0 112.2 jit_solution(5701204051186909690)
XLA Ops:
  0.6 0.7 add_select_fusion.1
  1.3 0.3 select_convert_fusion
  1.7 1.1 %maximum_bitcast_fusion = bf16[128,8,384]{2,1,0:T(8,128)(2,1)S(1)} fusion(bf16[1024,128]{1,0:T(8,128)(2,1)S(1)} %select_convert_fusion, bf16[1024,128]{1,0:T(8,128)(2,1)} %param.8, bf16[1024,128]{1,0:T(8,128)(2,1)} %param.7), kind=kLoop, calls=%fused_computation | loop fusion | flops 2359296 | bytes 1572864 | tf_op jit(solution)/shard_map/all_to_all | solution.py:236
  2.8 25.9 %all_to_all.22 = bf16[128,8,384]{2,1,0:T(8,128)(2,1)} all-to-all(bf16[128,8,384]{2,1,0:T(8,128)(2,1)S(1)} %maximum_bitcast_fusion), channel_id=1, replica_groups=mesh['ctx'=128] {'ctx'}, dimensions={0} | all-to-all | bytes 1572864 | tf_op jit(solution)/shard_map/all_to_all | solution.py:236
  28.7 0.0 copy-start.3
  28.7 6.0 %all-to-all-start = ((bf16[128,8,1024]{2,1,0:T(8,128)(2,1)}), bf16[128,8,1024]{2,1,0:T(8,128)(2,1)S(1)}, u32[]{:S(2)}, u32[]{:S(2)}) async-start(bf16[128,8,1024]{2,1,0:T(8,128)(2,1)} %bitcast.9), calls=%async_computation | async-start | bytes 4194304 | tf_op jit(solution)/shard_map/all_to_all | solution.py:236
  34.7 2.8 %place_kv.1 = (bf16[1024,256]{1,0:T(8,128)(2,1)}, s32[8,1024]{1,0:T(8,128)}) custom-call(bf16[1024,384]{1,0:T(8,128)(2,1)} %bitcast.8), custom_call_target="tpu_custom_call" | custom-call | tf_op jit(solution)/shard_map/place_kv/pallas_call | solution.py:60
  37.4 1.0 slice.27
  38.4 3.6 %collective-permute-start.1 = (bf16[512,256]{1,0:T(8,128)(2,1)S(1)}, bf16[512,256]{1,0:T(8,128)(2,1)S(1)}, u32[]{:S(2)}, u32[]{:S(2)}) collective-permute-start(bf16[512,256]{1,0:T(8,128)(2,1)S(1)} %slice.27), channel_id=1, source_target_pairs={{0,1},{1,2},{2,3},{3,4},{4,5},{5,6},{6,7},{7,8},{8,9},{9,10},{10,1... | collective-permute-start | bytes 786440 | tf_op jit(solution)/shard_map/ppermute | solution.py:36
  42.0 0.0 copy-done.3
  42.1 2.0 %collective-permute-start = (s32[512]{0:T(512)S(1)}, s32[512]{0:T(512)S(1)}, u32[]{:S(2)}, u32[]{:S(2)}) collective-permute-start(s32[512]{0:T(512)S(1)} %slice.26), channel_id=1, source_target_pairs={{0,1},{1,2},{2,3},{3,4},{4,5},{5,6},{6,7},{7,8},{8,9},{9,10},{10,1... | collective-permute-start | bytes 6152 | tf_op jit(solution)/shard_map/ppermute | solution.py:36
  44.1 16.1 %collective-permute-done = s32[512]{0:T(512)S(1)} collective-permute-done((s32[512]{0:T(512)S(1)}, s32[512]{0:T(512)S(1)}, u32[]{:S(2)}, u32[]{:S(2)}) %collective-permute-start) | collective-permute-done | bytes 2080 | tf_op jit(solution)/shard_map/ppermute | solution.py:36
  60.2 0.0 collective-permute-done.1.halo_ref
  60.2 3.8 %all-to-all-done = bf16[128,8,1024]{2,1,0:T(8,128)(2,1)S(1)} async-done(((bf16[128,8,1024]{2,1,0:T(8,128)(2,1)}), bf16[128,8,1024]{2,1,0:T(8,128)(2,1)S(1)}, u32[]{:S(2)}, u32[]{:S(2)}) %all-to-all-start) | async-done | bytes 2097184 | tf_op jit(solution)/shard_map/all_to_all | solution.py:236
  64.1 0.0 copy-start
  64.1 1.6 %copy-done = bf16[1024,1024]{1,0:T(8,128)(2,1)S(1)} copy-done((bf16[1024,1024]{1,0:T(8,128)(2,1)S(1)}, bf16[1024,1024]{1,0:T(8,128)(2,1)}, u32[]{:S(2)}) %copy-start) | copy-done | bytes 2097176
  65.7 0.0 copy-start.1
  65.7 1.0 copy-done.1
  66.7 0.8 copy-done.2
  67.5 35.2 %attend.1 = (bf16[1024,1024]{1,0:T(8,128)(2,1)}, f32[1024,1024]{1,0:T(8,128)}, f32[1536,128]{1,0:T(8,128)S(1)}, f32[1536,128]{1,0:T(8,128)S(1)}) custom-call(s32[1536]{0:T(1024)S(1)} %get-tuple-element.19.docs_smem, bf16[1024,1024]{1,0:T(8,128)(2,1)S(1)} %bitcast.7, s32[8,1024]{1,0:T(8,128)S(1)} %copy-done.2, bf16[1024,256]{1,0:T(8,128)(2,1)S(1)} %copy-done.1, ...), custom_call_target="tpu_custom_call" | custom-call | tf_op jit(solution)/shard_map/attend/pallas_call | solution.py:192
  102.7 1.9 %collective-permute-start.2 = (bf16[512,256]{1,0:T(8,128)(2,1)S(1)}, bf16[512,256]{1,0:T(8,128)(2,1)S(1)}, u32[]{:S(2)}, u32[]{:S(2)}) collective-permute-start(bf16[512,256]{1,0:T(8,128)(2,1)S(1)} %pad_maximum_fusion), channel_id=1, source_target_pairs={{1,0},{2,1},{3,2},{4,3},{5,4},{6,5},{7,6},{8,7},{9,8},{10,9},{11,1... | collective-permute-start | bytes 786440 | tf_op jit(solution)/shard_map/ppermute | solution.py:36
  104.7 5.8 %collective-permute-done.2 = bf16[512,256]{1,0:T(8,128)(2,1)S(1)} collective-permute-done((bf16[512,256]{1,0:T(8,128)(2,1)S(1)}, bf16[512,256]{1,0:T(8,128)(2,1)S(1)}, u32[]{:S(2)}, u32[]{:S(2)}) %collective-permute-start.2) | collective-permute-done | bytes 262176 | tf_op jit(solution)/shard_map/ppermute | solution.py:36
  110.5 0.9 pad_add_fusion.1
  111.3 0.9 pad_add_fusion
  (9 shorter events, 0.1 us)
Async XLA Ops:
  28.7 13.4 %copy-start.3 = (s32[1024]{0:T(1024)S(1)}, s32[1024]{0:T(1024)}, u32[]{:S(2)}) copy-start(s32[1024]{0:T(1024)} %param.10) | copy-start | bytes 12292
  28.7 35.4 %all-to-all-start = ((bf16[128,8,1024]{2,1,0:T(8,128)(2,1)}), bf16[128,8,1024]{2,1,0:T(8,128)(2,1)S(1)}, u32[]{:S(2)}, u32[]{:S(2)}) async-start(bf16[128,8,1024]{2,1,0:T(8,128)(2,1)} %bitcast.9), calls=%async_computation | async-start | bytes 4194304 | tf_op jit(solution)/shard_map/all_to_all | solution.py:236
  38.4 21.8 %collective-permute-start.1 = (bf16[512,256]{1,0:T(8,128)(2,1)S(1)}, bf16[512,256]{1,0:T(8,128)(2,1)S(1)}, u32[]{:S(2)}, u32[]{:S(2)}) collective-permute-start(bf16[512,256]{1,0:T(8,128)(2,1)S(1)} %slice.27), channel_id=1, source_target_pairs={{0,1},{1,2},{2,3},{3,4},{4,5},{5,6},{6,7},{7,8},{8,9},{9,10},{10,1... | collective-permute-start | bytes 786440 | tf_op jit(solution)/shard_map/ppermute | solution.py:36
  42.1 18.1 %collective-permute-start = (s32[512]{0:T(512)S(1)}, s32[512]{0:T(512)S(1)}, u32[]{:S(2)}, u32[]{:S(2)}) collective-permute-start(s32[512]{0:T(512)S(1)} %slice.26), channel_id=1, source_target_pairs={{0,1},{1,2},{2,3},{3,4},{4,5},{5,6},{6,7},{7,8},{8,9},{9,10},{10,1... | collective-permute-start | bytes 6152 | tf_op jit(solution)/shard_map/ppermute | solution.py:36
  64.1 1.6 %copy-start = (bf16[1024,1024]{1,0:T(8,128)(2,1)S(1)}, bf16[1024,1024]{1,0:T(8,128)(2,1)}, u32[]{:S(2)}) copy-start(bf16[1024,1024]{1,0:T(8,128)(2,1)} %grad_ref.1) | copy-start | bytes 6291460
  65.7 1.0 copy-start.1
  66.7 0.8 copy-start.2
  102.7 7.7 %collective-permute-start.2 = (bf16[512,256]{1,0:T(8,128)(2,1)S(1)}, bf16[512,256]{1,0:T(8,128)(2,1)S(1)}, u32[]{:S(2)}, u32[]{:S(2)}) collective-permute-start(bf16[512,256]{1,0:T(8,128)(2,1)S(1)} %pad_maximum_fusion), channel_id=1, source_target_pairs={{1,0},{2,1},{3,2},{4,3},{5,4},{6,5},{7,6},{8,7},{9,8},{10,9},{11,1... | collective-permute-start | bytes 786440 | tf_op jit(solution)/shard_map/ppermute | solution.py:36
